TPU v7x, 32 devices: a whole 2x2x4 slice. The times are simulated.
32 devices in a mesh: cfg: 2 (over y), space: 8 (over z, x), tm: 2 (over core).
Axes of the slice: x: 2, y: 2, z: 4, core: 2. Of those that a mesh axis runs over, the one named last changes fastest.
Arguments:
- eigvecs: bfloat16 [4, 2, 3, 1536, 256], P(('cfg', 'tm'), None, None, 'space'), parts along dimension 0, may hold values from -6 to 6
- momenta: int32 [3, 3], replicated, may hold values from -2 to 2, as said below
- pair_list: int32 [8, 2], P('tm'), may hold values from 0 to 1
- panels: bfloat16 [16, 2, 1024, 1024], P(('cfg', 'tm'), None, 'space'), parts along dimension 0, may hold values from -6 to 6
Outputs:
- dressed: bfloat16 [16, 3, 2, 1024, 1024], P(('cfg', 'tm'), None, None, 'space'), parts along dimension 0
There are 2 independent parts, one for each index of `cfg`. A program takes and returns all parts, laid end to end along the dimension named above; an argument that names none is the same for every part. Nothing has to cross between parts.
Inputs may be any that keep to these rules, and one draw needn't show every extreme that they name: `momenta`: the first component of every momentum is nonzero.
All inputs are finite; a program needn't handle non-finite values.
Results may differ from a plain program's by a relative error of at most 0.0075.
Values may be sent and summed in bfloat16 or wider, within the bound.
A program may use at most 64 MiB of HBM per device.

v0:
```python
import math
import jax
import jax.numpy as jnp
from jax import lax
from jax.sharding import PartitionSpec as P

LX = 64


def phased_block(cosine, sine_part, real_part, imag_part):
    cos_col = cosine[:, None]
    sin_col = sine_part[:, None]
    wave_re = cos_col * real_part + sin_col * imag_part
    wave_im = cos_col * imag_part - sin_col * real_part
    upper = jnp.concatenate([wave_re, wave_im], -1)
    lower = jnp.concatenate([wave_im, -wave_re], -1)
    return jnp.stack([upper, lower], -4).astype(jnp.bfloat16)


def local(eigvecs, momenta, pair_list, panels):
    slice_count, _, colors, slab_sites, vectors = eigvecs.shape
    mom_count = momenta.shape[0]
    space_count = lax.axis_size("space")
    first_site = lax.axis_index("space") * slab_sites
    site_index = first_site + jnp.arange(slab_sites, dtype=jnp.int32)
    xpos = site_index % LX
    ypos = site_index // LX % LX
    zpos = site_index // (LX * LX)
    wave = (
        momenta[:, 0:1] * xpos[None, :]
        + momenta[:, 1:2] * ypos[None, :]
        + momenta[:, 2:3] * zpos[None, :]
    )
    wave = jnp.mod(wave, LX)
    angle = wave.astype(jnp.float32) * jnp.float32(2.0 * math.pi / LX)
    cosine = jnp.cos(angle)
    sine_part = jnp.sin(angle)
    factor = 1.0 / math.sqrt(6.0 * slab_sites * space_count * vectors)
    real_part = eigvecs[:, 0].astype(jnp.float32)
    imag_part = eigvecs[:, 1].astype(jnp.float32)
    phased_all = jnp.concatenate(
        [
            phased_block(cosine[moment], sine_part[moment], real_part, imag_part)
            for moment in range(mom_count)
        ],
        -1,
    )
    phased_all = phased_all.reshape(slice_count, 2, colors, slab_sites, mom_count, 2 * vectors)
    gram_local = jnp.einsum(
        "trcsk,trcsml->tmkl", eigvecs, phased_all, preferred_element_type=jnp.float32
    )
    gram_local = factor * gram_local
    summed = lax.psum(gram_local, "space")
    own_fields = summed.astype(jnp.bfloat16)
    meson_fields = lax.all_gather(own_fields, "tm", axis=0, tiled=True)
    pair_count = pair_list.shape[0]
    panel_rows = panels.shape[2]
    panel_width = panels.shape[3]
    spins = panel_width // vectors
    source_fields = jnp.take(meson_fields, pair_list[:, 0], axis=0).reshape(
        pair_count, mom_count, vectors, 2, vectors
    )
    sink_fields = jnp.take(meson_fields, pair_list[:, 1], axis=0).reshape(
        pair_count, mom_count, vectors, 2, vectors
    )
    panel_parts = panels.reshape(pair_count, 2, panel_rows, spins, vectors)
    panel_re = panel_parts[:, 0]
    panel_im = panel_parts[:, 1]
    panel_mix = jnp.stack(
        [jnp.stack([panel_re, panel_im], 1), jnp.stack([panel_im, -panel_re], 1)], 1
    )
    right_dressed = jnp.einsum(
        "porxbk,pmlrk->pmoxbl", panel_mix, source_fields, preferred_element_type=jnp.float32
    )
    right_dressed = right_dressed.astype(jnp.bfloat16).reshape(
        pair_count * mom_count, 2, panel_rows, panel_width
    )
    turned = lax.all_to_all(right_dressed, "space", split_axis=3, concat_axis=2, tiled=True)
    column_count = turned.shape[3]
    turned = turned.reshape(pair_count, mom_count, 2, spins, vectors, column_count)
    turned_re = turned[:, :, 0]
    turned_im = turned[:, :, 1]
    mixed_parts = jnp.stack(
        [jnp.stack([turned_re, -turned_im], 2), jnp.stack([turned_im, turned_re], 2)], 2
    )
    dressed = jnp.einsum(
        "pmorajc,pmkrj->pmocak", mixed_parts, sink_fields, preferred_element_type=jnp.float32
    )
    return dressed.reshape(pair_count, mom_count, 2, column_count, panel_width).astype(jnp.bfloat16)


def solution(mesh):
    placed = (
        P(("cfg", "tm"), None, None, "space", None),
        P(),
        P("tm", None),
        P(("cfg", "tm"), None, "space", None),
    )
    return jax.shard_map(
        local,
        mesh=mesh,
        in_specs=placed,
        out_specs=P(("cfg", "tm"), None, None, "space", None),
        check_vma=False,
    )
```

profile of v0, /device:TPU:0, one launch (start us, length us, event | category | flops | bytes accessed | tf_op | source)
XLA Modules:
  0.0 343.8 jit_solution(5193341892418195743)
XLA Ops:
  6.5 0.0 all-gather.2.cloned.1.call-start
  6.6 1.0 slice_reduce_fusion.2
  7.6 0.1 fusion.37
  7.7 0.0 copy-start.3
  7.8 1.6 fusion.30
  9.3 0.1 maximum_bitcast_fusion.9
  9.4 0.1 pad_maximum_fusion
  9.5 0.0 copy-done.3
  9.6 0.3 fusion.28
  9.8 0.1 maximum_bitcast_fusion.11
  10.0 0.1 maximum_bitcast_fusion.13
  10.1 1.2 fusion.17
  11.3 83.3 %all-reduce.1 = bf16[1,3,256,512]{2,3,1,0:T(8,128)(2,1)S(1)} all-reduce(f32[1,3,256,512]{2,3,1,0:T(8,128)S(1)} %fusion.17), channel_id=1, replica_groups=mesh['cfg'=2,'space'=8,'tm'=2] {'space'}, use_global_device_ids=true, to_apply=%region_0.1 | all-reduce | flops 393216 | bytes 2359296 | tf_op jit(solution)/shard_map/psum | solution.py:53
  94.7 1.3 copy.48
  95.9 0.0 all-gather.2.cloned.1.call-update
  95.9 3.0 copy.49
  99.0 1.5 fusion.42
  100.4 1.5 copy.77
  102.0 1.2 neg.44
  103.2 0.0 copy-start.4
  103.2 0.0 copy-start.2
  103.2 2.4 copy.76
  105.6 2.3 copy.53
  107.9 0.0 copy-done.4
  107.9 0.0 copy-done.2
  107.9 2.7 maximum_bitcast_fusion.6
  110.7 0.0 all-gather.2.cloned.1.call-done
  110.7 2.2 gather_fusion.1
  112.8 2.0 broadcast_select_fusion
  114.9 3.8 %reshape.415 = bf16[4,3,256,2,256]{4,3,2,1,0:T(2,128)(2,1)S(1)} reshape(bf16[4,3,256,512]{3,2,1,0:T(8,128)(2,1)} %broadcast_select_fusion) | data formatting | bytes 6291456 | tf_op jit(solution)/shard_map/reshape | solution.py:60
  118.6 6.2 %bitcast_convert_fusion.1 = bf16[4,3,256,2,128,4]{4,2,5,3,1,0:T(8,128)(2,1)S(1)} fusion(bf16[4,1,2,128,4,256]{5,3,2,4,1,0:T(8,128)(2,1)} %maximum_bitcast_fusion.6, bf16[4,1,2,128,4,256]{5,3,2,4,1,0:T(8,128)(2,1)} %copy.53, bf16[4,3,256,2,256,1,1]{4,3,2,1,0,6,5:T(2,128)(2,1)S(1)} %bitcast.120), kind=kOutput, calls=%fused_computation.7 | convolution fusion | flops 3232759808 | bytes 13631488 | tf_op jit(solution)/shard_map/porxbk,pmlrk->pmoxbl/dot_general | solution.py:72
  124.8 36.6 %copy.55 = bf16[12,2,128,1024]{2,1,0,3:T(2,128)(2,1)} copy(bf16[12,2,128,1024]{2,3,1,0:T(8,128)(2,1)S(1)} %bitcast.117) | data formatting | bytes 12582912 | tf_op jit(solution)/shard_map/reshape | solution.py:75
  161.5 0.0 copy-start.1
  161.5 5.1 %all-to-all-start = ((bf16[12,2,128,1024]{2,1,0,3:T(2,128)(2,1)}), bf16[12,2,128,1024]{2,1,0,3:T(2,128)(2,1)}, u32[]{:S(2)}, u32[]{:S(2)}) async-start(bf16[12,2,128,1024]{2,1,0,3:T(2,128)(2,1)} %copy.55), calls=%async_computation | async-start | bytes 12582912 | tf_op jit(solution)/shard_map/all_to_all | solution.py:78
  166.5 0.0 copy-done.1
  166.6 2.5 gather_fusion
  169.0 2.3 broadcast_select_fusion.1
  171.3 3.1 reshape.414
  174.3 125.2 %all-to-all-done = bf16[12,2,128,1024]{2,1,0,3:T(2,128)(2,1)} async-done(((bf16[12,2,128,1024]{2,1,0,3:T(2,128)(2,1)}), bf16[12,2,128,1024]{2,1,0,3:T(2,128)(2,1)}, u32[]{:S(2)}, u32[]{:S(2)}) %all-to-all-start) | async-done | bytes 6291488 | tf_op jit(solution)/shard_map/all_to_all | solution.py:78
  299.6 6.9 %copy.56 = bf16[12,2,128,1024]{2,3,1,0:T(8,128)(2,1)} copy(bf16[12,2,128,1024]{2,1,0,3:T(2,128)(2,1)} %all-to-all-done) | data formatting | bytes 12582912 | tf_op jit(solution)/shard_map/all_to_all | solution.py:78
  306.4 8.6 %copy.57 = bf16[12,2,8,128,128]{4,3,2,1,0:T(8,128)(2,1)} copy(bf16[12,2,8,128,128]{3,4,2,1,0:T(8,128)(2,1)} %bitcast.114) | data formatting | bytes 12582912 | tf_op jit(solution)/shard_map/all_to_all | solution.py:78
  315.1 0.0 copy-start
  315.1 3.4 slice_bitcast_fusion
  318.5 1.2 copy-done
  319.7 0.4 fusion.41
  320.1 1.0 maximum_bitcast_fusion
  321.1 7.2 %bitcast_convert_fusion = bf16[4,3,256,2,4,128]{5,2,4,3,1,0:T(8,128)(2,1)} fusion(bf16[4,3,1,2,4,256,128]{6,5,3,4,2,1,0:T(8,128)(2,1)S(1)} %get-tuple-element.16, bf16[4,3,1,2,4,256,128]{6,5,3,4,2,1,0:T(8,128)(2,1)S(1)} %get-tuple-element.15, bf16[4,3,256,2,256,1,1]{4,3,2,1,0,6,5:T(2,128)(2,1)} %bitcast.119), kind=kOutput, calls=%fused_computation.6 | convolution fusion | flops 3249537024 | bytes 22020096 | tf_op jit(solution)/shard_map/pmorajc,pmkrj->pmocak/dot_general | solution.py:86
  328.3 8.6 %copy.62 = bf16[4,3,2,128,1024]{4,3,2,1,0:T(8,128)(2,1)} copy(bf16[4,3,2,128,1024]{3,4,2,1,0:T(8,128)(2,1)} %bitcast.118) | data formatting | bytes 12582912 | tf_op jit(solution)/shard_map/convert_element_type | solution.py:89
  (6 shorter events, 0.1 us)
Async XLA Ops:
  6.5 104.1 %all-gather.2.cloned.1.call-start = ((), (), s32[]{:S(2)}) async-start(), calls=%async_computation.1 | async-start | bytes 2359296 | tf_op jit(solution)/shard_map/all_gather | solution.py:55
  7.7 1.8 copy-start.3
  103.2 4.7 %copy-start.4 = (s32[4,2]{0,1:T(2,128)S(1)}, s32[4,2]{0,1:T(2,128)}, u32[]{:S(2)}) copy-start(s32[4,2]{0,1:T(2,128)} %param.8) | copy-start | bytes 100
  103.2 4.7 %copy-start.2 = (bf16[4,1,128,4,256]{4,2,1,3,0:T(8,128)(2,1)S(1)}, bf16[4,1,128,4,256]{4,2,1,3,0:T(8,128)(2,1)}, u32[]{:S(2)}) copy-start(bf16[4,1,128,4,256]{4,2,1,3,0:T(8,128)(2,1)} %neg.44) | copy-start | bytes 3145732
  161.5 5.1 %copy-start.1 = (bf16[2,3,256,512]{3,2,1,0:T(8,128)(2,1)S(1)}, bf16[2,3,256,512]{3,2,1,0:T(8,128)(2,1)}, u32[]{:S(2)}) copy-start(bf16[2,3,256,512]{3,2,1,0:T(8,128)(2,1)} %all-gather.2.cloned.1.call-done) | copy-start | bytes 4718596
  161.5 138.1 %all-to-all-start = ((bf16[12,2,128,1024]{2,1,0,3:T(2,128)(2,1)}), bf16[12,2,128,1024]{2,1,0,3:T(2,128)(2,1)}, u32[]{:S(2)}, u32[]{:S(2)}) async-start(bf16[12,2,128,1024]{2,1,0,3:T(2,128)(2,1)} %copy.55), calls=%async_computation | async-start | bytes 12582912 | tf_op jit(solution)/shard_map/all_to_all | solution.py:78
  315.1 4.6 %copy-start = (bf16[12,2,8,128,128]{4,3,2,1,0:T(8,128)(2,1)S(1)}, bf16[12,2,8,128,128]{4,3,2,1,0:T(8,128)(2,1)}, u32[]{:S(2)}) copy-start(bf16[12,2,8,128,128]{4,3,2,1,0:T(8,128)(2,1)} %copy.57) | copy-start | bytes 18874372
Sparse Core Ops, SparseCore 0:
  96.1 7.9 all-gather.1
where the time goes:
time: 345 us; the launch traced here: 344 us
  waiting for transfers between devices  125 us (36%)
  local copies, waits for them, and re-layouts  89.8 us (26%)
  blocking collectives  83.3 us (24%)
  matrix products  14.6 us (4%)
  between operations  13.6 us (4%)
  other arithmetic  12 us (3%)
  starting transfers between devices  5.08 us (1%)
    all_to_all x1, waiting for transfers between devices, local(): lax.all_to_all(right_dressed, 'space', split_axis=3, concat_axis=2, tiled...  125 us
    psum x1, blocking collectives, local(): summed = lax.psum(gram_local, 'space')  83.3 us
    reshape x1, local copies, waits for them, and re-layouts, local(): right_dressed.astype(jnp.bfloat16)  36.6 us
    all_to_all x2, local copies, waits for them, and re-layouts, local(): lax.all_to_all(right_dressed, 'space', split_axis=3, concat_axis=2, tiled...  15.5 us
    unnamed x14, local copies, waits for them, and re-layouts  11.6 us
    convert_element_type x1, local copies, waits for them, and re-layouts, local(): dressed.reshape(pair_count, mom_count, 2, column_count, panel_width)  8.62 us
    dot_general x1, matrix products, local(): jnp.einsum('pmorajc,pmkrj->pmocak', mixed_parts, sink_fields, preferred_e...  7.2 us
  transfers between devices with their start and end apart: 2, of which 1 were waited for; matrix products, arithmetic and copies ran while one was open for 7% of the time, Pallas kernels for 0%

commit v1 on v0

--- a/solution.py
+++ b/solution.py
@@ -75,7 +75,12 @@
     right_dressed = right_dressed.astype(jnp.bfloat16).reshape(
         pair_count * mom_count, 2, panel_rows, panel_width
     )
-    turned = lax.all_to_all(right_dressed, "space", split_axis=3, concat_axis=2, tiled=True)
+    turned = jnp.concatenate(
+        lax.all_to_all(
+            jnp.stack(jnp.split(right_dressed, lax.axis_size("space"), axis=3)), "space", 0, 0
+        ),
+        axis=2,
+    )
     column_count = turned.shape[3]
     turned = turned.reshape(pair_count, mom_count, 2, spins, vectors, column_count)
     turned_re = turned[:, :, 0]

time: 345 us -> 317 us (0.919)
  local copies, waits for them, and re-layouts: 89.8 us -> 64.3 us
    reshape x1 -> x0, local copies, waits for them, and re-layouts: 36.6 us -> none  [local(): right_dressed.astype(jnp.bfloat16)]
    unnamed x14 -> x33, local copies, waits for them, and re-layouts: 11.6 us -> 30 us
    all_to_all x2 -> x1, local copies, waits for them, and re-layouts: 15.5 us -> 4.14 us  [local(): lax.all_to_all(jnp.stack(jnp.split(right_dressed, lax.axis_size('space'),...]
where the time goes in v1:
time: 317 us; the launch traced here: 316 us
  waiting for transfers between devices  125 us (39%)
  blocking collectives  83.3 us (26%)
  local copies, waits for them, and re-layouts  64.3 us (20%)
  between operations  13.7 us (4%)
  matrix products  12.8 us (4%)
  other arithmetic  12.1 us (4%)
  starting transfers between devices  5.08 us (2%)
    all_to_all x1, waiting for transfers between devices, local(): lax.all_to_all(jnp.stack(jnp.split(right_dressed, lax.axis_size('space'),...  125 us
    psum x1, blocking collectives, local(): summed = lax.psum(gram_local, 'space')  83.3 us
    unnamed x33, local copies, waits for them, and re-layouts  30 us
    convert_element_type x1, local copies, waits for them, and re-layouts, local(): dressed.reshape(pair_count, mom_count, 2, column_count, panel_width)  8.62 us
  transfers between devices with their start and end apart: 2, of which 1 were waited for; matrix products, arithmetic and copies ran while one was open for 7% of the time, Pallas kernels for 0%

profile of v1, /device:TPU:0, one launch (start us, length us, event | category | flops | bytes accessed | tf_op | source)
XLA Modules:
  0.0 316.4 jit_solution(9828272889111505163)
XLA Ops:
  6.6 1.0 slice_reduce_fusion.2
  7.6 0.1 fusion.37
  7.8 1.6 fusion.30
  9.4 0.1 pad_maximum_fusion
  9.6 0.3 fusion.28
  10.1 1.2 fusion.17
  11.3 83.3 %all-reduce.1 = bf16[1,3,256,512]{2,3,1,0:T(8,128)(2,1)S(1)} all-reduce(f32[1,3,256,512]{2,3,1,0:T(8,128)S(1)} %fusion.17), channel_id=1, replica_groups=mesh['cfg'=2,'space'=8,'tm'=2] {'space'}, use_global_device_ids=true, to_apply=%region_0.1 | all-reduce | flops 393216 | bytes 2359296 | tf_op jit(solution)/shard_map/psum | solution.py:53
  94.7 1.2 copy.40
  95.9 3.0 copy.41
  99.0 1.5 fusion.43
  100.4 1.5 copy.75
  101.9 1.2 neg.44
  103.2 2.4 copy.74
  105.5 2.4 copy.45
  107.9 2.8 maximum_bitcast_fusion.6
  110.7 2.2 gather_fusion.1
  112.9 2.0 broadcast_select_fusion
  114.9 3.8 %reshape.414 = bf16[4,3,256,2,256]{4,3,2,1,0:T(2,128)(2,1)S(1)} reshape(bf16[4,3,256,512]{3,2,1,0:T(8,128)(2,1)} %broadcast_select_fusion) | data formatting | bytes 6291456 | tf_op jit(solution)/shard_map/reshape | solution.py:60
  118.7 6.2 %bitcast_convert_fusion.1 = bf16[4,3,256,2,128,4]{4,2,5,3,1,0:T(8,128)(2,1)S(1)} fusion(bf16[4,1,2,128,4,256]{5,3,2,4,1,0:T(8,128)(2,1)} %maximum_bitcast_fusion.6, bf16[4,1,2,128,4,256]{5,3,2,4,1,0:T(8,128)(2,1)} %copy.45, bf16[4,3,256,2,256,1,1]{4,3,2,1,0,6,5:T(2,128)(2,1)S(1)} %bitcast.134), kind=kOutput, calls=%fused_computation.7 | convolution fusion | flops 3232759808 | bytes 13631488 | tf_op jit(solution)/shard_map/porxbk,pmlrk->pmoxbl/dot_general | solution.py:72
  124.9 3.1 fusion.42
  128.0 2.3 copy.76
  130.3 2.1 bitcast_dynamic-update-slice_fusion.7
  132.4 2.3 copy.77
  134.7 2.3 copy.78
  137.0 2.3 copy.79
  139.3 1.2 copy.80
  140.5 0.4 copy.81
  140.9 0.4 copy.82
  141.2 0.4 copy.83
  141.7 2.2 bitcast_dynamic-update-slice_fusion.6
  143.9 2.1 bitcast_dynamic-update-slice_fusion.5
  146.0 1.0 bitcast_dynamic-update-slice_fusion.4
  146.9 1.0 bitcast_dynamic-update-slice_fusion.3
  147.9 0.9 bitcast_dynamic-update-slice_fusion.2
  148.8 0.9 bitcast_dynamic-update-slice_fusion.1
  149.7 0.9 bitcast_dynamic-update-slice_fusion
  150.7 5.1 %all-to-all-start = ((bf16[8,12,2,128,128]{4,3,2,1,0:T(8,128)(2,1)}), bf16[8,12,2,128,128]{4,3,2,1,0:T(8,128)(2,1)}, u32[]{:S(2)}, u32[]{:S(2)}) async-start(bf16[8,12,2,128,128]{4,3,2,1,0:T(8,128)(2,1)} %bitcast_dynamic-update-slice_fusion), calls=%async_computation | async-start | bytes 12582912 | tf_op jit(solution)/shard_map/all_to_all | solution.py:79
  155.8 2.5 gather_fusion
  158.2 2.3 broadcast_select_fusion.1
  160.5 3.1 reshape.413
  163.5 125.2 %all-to-all-done = bf16[8,12,2,128,128]{4,3,2,1,0:T(8,128)(2,1)} async-done(((bf16[8,12,2,128,128]{4,3,2,1,0:T(8,128)(2,1)}), bf16[8,12,2,128,128]{4,3,2,1,0:T(8,128)(2,1)}, u32[]{:S(2)}, u32[]{:S(2)}) %all-to-all-start) | async-done | bytes 6291488 | tf_op jit(solution)/shard_map/all_to_all | solution.py:79
  288.7 4.1 %copy.55 = bf16[8,12,2,128,128]{4,3,0,2,1:T(8,128)(2,1)S(1)} copy(bf16[8,12,2,128,128]{4,3,2,1,0:T(8,128)(2,1)} %all-to-all-done) | data formatting | bytes 12582912 | tf_op jit(solution)/shard_map/all_to_all | solution.py:79
  292.9 0.4 slice_bitcast_fusion
  293.3 0.4 fusion.41
  293.7 1.0 maximum_bitcast_fusion
  294.7 0.9 copy-done.2
  295.6 5.3 %bitcast_convert_fusion = bf16[4,3,256,2,4,128]{5,2,4,3,1,0:T(8,128)(2,1)} fusion(bf16[4,3,1,2,4,256,128]{6,5,3,4,2,1,0:T(8,128)(2,1)S(1)} %get-tuple-element.24, bf16[4,3,1,2,4,256,128]{6,5,3,4,2,1,0:T(8,128)(2,1)S(1)} %get-tuple-element.23, bf16[4,3,256,2,256,1,1]{4,3,2,1,0,6,5:T(2,128)(2,1)S(1)} %bitcast.133), kind=kOutput, calls=%fused_computation.6 | convolution fusion | flops 3249537024 | bytes 22020096 | tf_op jit(solution)/shard_map/pmorajc,pmkrj->pmocak/dot_general | solution.py:91
  300.9 8.6 %copy.60 = bf16[4,3,2,128,1024]{4,3,2,1,0:T(8,128)(2,1)} copy(bf16[4,3,2,128,1024]{3,4,2,1,0:T(8,128)(2,1)} %bitcast.132) | data formatting | bytes 12582912 | tf_op jit(solution)/shard_map/convert_element_type | solution.py:94
  (25 shorter events, 0.4 us)
Async XLA Ops:
  6.5 104.2 %all-gather.2.cloned.1.call-start = ((), (), s32[]{:S(2)}) async-start(), calls=%async_computation.1 | async-start | bytes 2359296 | tf_op jit(solution)/shard_map/all_gather | solution.py:55
  7.7 1.8 copy-start.5
  103.2 4.7 %copy-start.6 = (s32[4,2]{0,1:T(2,128)S(1)}, s32[4,2]{0,1:T(2,128)}, u32[]{:S(2)}) copy-start(s32[4,2]{0,1:T(2,128)} %param.8) | copy-start | bytes 100
  103.2 4.8 %copy-start.1 = (bf16[4,1,128,4,256]{4,2,1,3,0:T(8,128)(2,1)S(1)}, bf16[4,1,128,4,256]{4,2,1,3,0:T(8,128)(2,1)}, u32[]{:S(2)}) copy-start(bf16[4,1,128,4,256]{4,2,1,3,0:T(8,128)(2,1)} %neg.44) | copy-start | bytes 3145732
  141.6 4.3 %copy-start.4 = (bf16[12,2,128,128]{3,2,1,0:T(8,128)(2,1)S(1)}, bf16[12,2,128,128]{3,2,1,0:T(8,128)(2,1)}, u32[]{:S(2)}) copy-start(bf16[12,2,128,128]{3,2,1,0:T(8,128)(2,1)} %copy.79) | copy-start | bytes 2359300
  141.6 5.3 %copy-start.3 = (bf16[12,2,128,128]{3,2,1,0:T(8,128)(2,1)S(1)}, bf16[12,2,128,128]{3,2,1,0:T(8,128)(2,1)}, u32[]{:S(2)}) copy-start(bf16[12,2,128,128]{3,2,1,0:T(8,128)(2,1)} %copy.80) | copy-start | bytes 2359300
  150.7 5.1 %copy-start = (bf16[2,3,256,512]{3,2,1,0:T(8,128)(2,1)S(1)}, bf16[2,3,256,512]{3,2,1,0:T(8,128)(2,1)}, u32[]{:S(2)}) copy-start(bf16[2,3,256,512]{3,2,1,0:T(8,128)(2,1)} %all-gather.2.cloned.1.call-done) | copy-start | bytes 4718596
  150.7 138.0 %all-to-all-start = ((bf16[8,12,2,128,128]{4,3,2,1,0:T(8,128)(2,1)}), bf16[8,12,2,128,128]{4,3,2,1,0:T(8,128)(2,1)}, u32[]{:S(2)}, u32[]{:S(2)}) async-start(bf16[8,12,2,128,128]{4,3,2,1,0:T(8,128)(2,1)} %bitcast_dynamic-update-slice_fusion), calls=%async_computation | async-start | bytes 12582912 | tf_op jit(solution)/shard_map/all_to_all | solution.py:79
  293.7 1.9 copy-start.2
Sparse Core Ops, SparseCore 0:
  96.0 7.9 all-gather.1
